TPU v7x, 32 devices: a whole 2x2x4 slice. The times are simulated.
32 devices in a mesh: groups: 2 (over y), dp: 4 (over z), landmark: 4 (over x, core).
Axes of the slice: x: 2, y: 2, z: 4, core: 2. Of those that a mesh axis runs over, the one named last changes fastest.
Arguments:
- images: bfloat16 [256, 1024], P(('groups', 'dp')), parts along dimension 0, may hold values from -6 to 6, as said below
- captions: bfloat16 [256, 768], P(('groups', 'dp')), parts along dimension 0, may hold values from -6 to 6, as said below
- caption_of: int32 [256], P(('groups', 'dp')), parts along dimension 0, may hold values from 0 to 31, as said below
- image_landmarks: bfloat16 [16384, 1024], P(('landmark', 'dp')), may hold values from -6 to 6
- image_gamma: float32 [16384], P(('landmark', 'dp')), may hold values from 8 to 40
- text_landmarks: bfloat16 [4096, 768], P(('dp', 'landmark')), may hold values from -6 to 6
- text_gamma: float32 [4096], P(('dp', 'landmark')), may hold values from 8 to 40
Outputs:
- zstat: float32 [32768, 4096], P(('groups', 'landmark'), 'dp'), parts along dimension 0
- image_mean: float32 [32768], P(('groups', 'landmark', 'dp')), parts along dimension 0
- text_mean: float32 [8192], P(('groups', 'dp', 'landmark')), parts along dimension 0
There are 2 independent parts, one for each index of `groups`. A program takes and returns all parts, laid end to end along the dimension named above; an argument that names none is the same for every part. Nothing has to cross between parts.
Inputs may be any that keep to these rules, and one draw needn't show every extreme that they name: `caption_of`: within each aligned block of 32 rows (the pairs of one index of dp) the values are a permutation of 0 to 31. `images`: image rows are embeddings; no row is zero. `captions`: caption rows are embeddings; no row is zero.
All inputs are finite; a program needn't handle non-finite values.
Results may differ from a plain program's by a relative error of at most 0.03.
Values may be sent and summed in bfloat16 or wider, within the bound.
A program may use at most 128 MiB of HBM per device.

v0:
```python
import jax
import jax.numpy as jnp
from jax import lax
from jax.sharding import PartitionSpec as P


def unit_rows(values):
    wide = values.astype(jnp.float32)
    return wide * lax.rsqrt(jnp.sum(wide * wide, axis=-1, keepdims=True) + 1e-06)


def features(left, right):
    inner = lax.dot_general(
        left, right, (((1,), (1,)), ((), ())), preferred_element_type=jnp.float32
    )
    return jnp.exp(inner).astype(jnp.bfloat16)


def per_device(
    images, captions, caption_of, image_landmarks, image_gamma, text_landmarks, text_gamma
):
    paired = jnp.take(captions, caption_of, axis=0)
    image_unit = unit_rows(images).astype(jnp.bfloat16)
    caption_unit = unit_rows(paired).astype(jnp.bfloat16)
    own_image_keys = (unit_rows(image_landmarks) * image_gamma[:, None]).astype(jnp.bfloat16)
    own_text_keys = (unit_rows(text_landmarks) * text_gamma[:, None]).astype(jnp.bfloat16)
    text_keys = lax.all_gather(own_text_keys, "landmark", axis=0, tiled=True)
    block_rows = images.shape[0]
    pair_count = block_rows * lax.axis_size("dp")
    image_keys = lax.all_gather(own_image_keys, "dp", axis=0, tiled=True)
    image_part = lax.all_gather(image_unit, "dp", axis=0, tiled=True)
    caption_part = lax.all_gather(caption_unit, "dp", axis=0, tiled=True)
    image_store = features(image_part, image_keys)
    text_store = features(caption_part, text_keys)
    image_mean = jnp.mean(image_store, axis=0, dtype=jnp.float32)
    text_mean = jnp.mean(text_store, axis=0, dtype=jnp.float32)
    image_dev = image_store.astype(jnp.float32) - image_mean
    text_dev = text_store.astype(jnp.float32) - text_mean
    image_var = jnp.mean(image_dev * image_dev, axis=0)
    text_var = jnp.mean(text_dev * text_dev, axis=0)
    moment = (
        lax.dot_general(
            image_store, text_store, (((0,), (0,)), ((), ())), preferred_element_type=jnp.float32
        )
        / pair_count
    )
    centred = moment - image_mean[:, None] * text_mean[None, :]
    zstat = (
        jnp.sqrt(jnp.float32(pair_count))
        * centred
        * lax.rsqrt(image_var + 1e-06)[:, None]
        * lax.rsqrt(text_var + 1e-06)[None, :]
    )
    image_width = own_image_keys.shape[0]
    text_width = own_text_keys.shape[0]
    image_part_mean = lax.dynamic_slice_in_dim(
        image_mean, lax.axis_index("dp") * image_width, image_width
    )
    text_part_mean = lax.dynamic_slice_in_dim(
        text_mean, lax.axis_index("landmark") * text_width, text_width
    )
    return (zstat, image_part_mean, text_part_mean)


def solution(mesh):
    in_specs = (
        P(("groups", "dp"), None),
        P(("groups", "dp"), None),
        P(("groups", "dp")),
        P(("landmark", "dp"), None),
        P(("landmark", "dp")),
        P(("dp", "landmark"), None),
        P(("dp", "landmark")),
    )
    out_specs = (
        P(("groups", "landmark"), "dp"),
        P(("groups", "landmark", "dp")),
        P(("groups", "dp", "landmark")),
    )
    return jax.shard_map(
        per_device, mesh=mesh, in_specs=in_specs, out_specs=out_specs, check_vma=False
    )
```

profile of v0, /device:TPU:0, one launch (start us, length us, event | category | flops | bytes accessed | tf_op | source)
XLA Modules:
  0.0 206.6 jit_solution(16714608103492476143)
XLA Ops:
  7.2 0.0 copy-start
  7.2 0.0 copy-start.1
  7.2 0.0 all-gather.5.cloned.1.call-start
  7.2 1.3 fusion.7
  8.5 2.0 fusion.9
  10.5 0.0 all-gather.5.cloned.1.call-update
  10.5 0.0 copy-start.3
  10.5 0.0 copy-start.2
  10.6 0.0 all-gather.3.cloned.1.call-start
  10.6 2.1 %fusion.1 = f32[1024]{0:T(1024)S(1)} fusion(bf16[1024,1024]{1,0:T(8,128)(2,1)} %param.10), kind=kLoop, calls=%fused_computation.6 | loop fusion | flops 3144704 | bytes 2101248 | tf_op jit(solution)/shard_map/reduce_sum | solution.py:9
  12.7 0.0 copy-done.1
  12.7 2.6 %fusion.3 = bf16[1024,1024]{1,0:T(8,128)(2,1)} fusion(bf16[1024,1024]{1,0:T(8,128)(2,1)S(1)} %copy-done.1, f32[1024]{0:T(1024)} %param.11, f32[1024]{0:T(1024)S(1)} %add_rsqrt_fusion.1), kind=kLoop, calls=%fused_computation.8 | loop fusion | flops 4194304 | bytes 4202496 | tf_op jit(solution)/shard_map/convert_element_type | solution.py:25
  15.2 0.0 all-gather.3.cloned.1.call-update
  15.3 0.0 copy-done.3
  15.3 0.0 copy-done
  15.3 0.6 gather_fusion
  16.0 0.2 fusion.14
  16.2 0.1 fusion.15
  16.3 15.3 %all_gather.14 = bf16[128,768]{1,0:T(8,128)(2,1)S(1)} all-gather(bf16[32,768]{1,0:T(8,128)(2,1)S(1)} %fusion.15), channel_id=1, replica_groups=mesh['groups'=2,'dp'=4,'landmark'=4] {'dp'}, dimensions={0}, use_global_device_ids=true | all-gather | bytes 245760 | tf_op jit(solution)/shard_map/all_gather | solution.py:32
  31.6 0.0 copy-done.2
  31.6 0.1 fusion.12
  31.7 0.1 fusion.13
  31.8 14.3 %all_gather.12 = bf16[128,1024]{1,0:T(8,128)(2,1)S(1)} all-gather(bf16[32,1024]{1,0:T(8,128)(2,1)S(1)} %fusion.13), channel_id=1, replica_groups=mesh['groups'=2,'dp'=4,'landmark'=4] {'dp'}, dimensions={0}, use_global_device_ids=true | all-gather | bytes 327680 | tf_op jit(solution)/shard_map/all_gather | solution.py:31
  46.1 0.0 all-gather.5.cloned.1.call-done
  46.1 2.2 %convert_reduce_fusion.1 = (f32[1024]{0:T(1024)S(1)}, bf16[128,1024]{1,0:T(8,128)(2,1)S(1)}) fusion(bf16[128,768]{1,0:T(8,128)(2,1)S(1)} %all_gather.14, bf16[1024,768]{1,0:T(8,128)(2,1)} %all-gather.5.cloned.1.call-done), kind=kOutput, calls=%fused_computation.21 | convolution fusion | flops 201718784 | bytes 2035712 | tf_op jit(solution)/shard_map/dot_general | solution.py:13
  48.4 0.6 dynamic_slice.7
  49.0 0.1 fusion.11
  49.1 135.7 %all-gather.3.cloned.1.call-done = bf16[4096,1024]{1,0:T(8,128)(2,1)} async-done(((bf16[1024,1024]{1,0:T(8,128)(2,1)}), bf16[4096,1024]{1,0:T(8,128)(2,1)}) %all-gather.3.cloned.1.call-update) | async-done | bytes 8388624 | tf_op jit(solution)/shard_map/all_gather | solution.py:30
  184.9 6.3 %convert_reduce_fusion = (f32[4096]{0:T(1024)S(1)}, bf16[128,4096]{1,0:T(8,128)(2,1)S(1)}) fusion(bf16[128,1024]{1,0:T(8,128)(2,1)S(1)} %all_gather.12, bf16[4096,1024]{1,0:T(8,128)(2,1)} %all-gather.3.cloned.1.call-done), kind=kOutput, calls=%fused_computation.10 | convolution fusion | flops 1075310592 | bytes 9715712 | tf_op jit(solution)/shard_map/dot_general | solution.py:13
  191.2 0.3 fusion.5
  191.5 0.6 dynamic_slice.6
  192.1 7.7 %multiply_multiply_fusion = f32[4096,1024]{1,0:T(8,128)} fusion(bf16[128,4096]{1,0:T(8,128)(2,1)S(1)} %get-tuple-element.6, bf16[128,1024]{1,0:T(8,128)(2,1)S(1)} %get-tuple-element.4, f32[1024]{0:T(1024)S(1)} %add_rsqrt_fusion, f32[4096]{0:T(1024)S(1)} %rsqrt_multiply_fusion, f32[1024]{0:T(1024)S(1)} %broadcast_multiply_fusion.1, ...), kind=kOutput, calls=%fused_computation.1 | convolution fusion | flops 1094713344 | bytes 18128896 | tf_op jit(solution)/shard_map/dot_general | solution.py:42
  (11 shorter events, 0.1 us)
Async XLA Ops:
  7.2 8.2 %copy-start = (bf16[32,768]{1,0:T(8,128)(2,1)S(1)}, bf16[32,768]{1,0:T(8,128)(2,1)}, u32[]{:S(2)}) copy-start(bf16[32,768]{1,0:T(8,128)(2,1)} %param.8) | copy-start | bytes 147460
  7.2 5.5 %copy-start.1 = (bf16[1024,1024]{1,0:T(8,128)(2,1)S(1)}, bf16[1024,1024]{1,0:T(8,128)(2,1)}, u32[]{:S(2)}) copy-start(bf16[1024,1024]{1,0:T(8,128)(2,1)} %param.10) | copy-start | bytes 6291460
  7.2 38.9 %all-gather.5.cloned.1.call-start = ((), (), s32[]{:S(2)}) async-start(), calls=%async_computation.1 | async-start | bytes 1966080 | tf_op jit(solution)/shard_map/all_gather | solution.py:27
  10.5 4.8 %copy-start.3 = (s32[32]{0:T(128)S(1)}, s32[32]{0:T(128)}, u32[]{:S(2)}) copy-start(s32[32]{0:T(128)} %param.9) | copy-start | bytes 388
  10.5 21.1 %copy-start.2 = (bf16[32,1024]{1,0:T(8,128)(2,1)S(1)}, bf16[32,1024]{1,0:T(8,128)(2,1)}, u32[]{:S(2)}) copy-start(bf16[32,1024]{1,0:T(8,128)(2,1)} %param.7) | copy-start | bytes 196612
  10.6 174.3 %all-gather.3.cloned.1.call-start = ((), (), s32[]{:S(2)}) async-start(), calls=%async_computation | async-start | bytes 10485760 | tf_op jit(solution)/shard_map/all_gather | solution.py:30
Sparse Core Ops, SparseCore 0:
  10.6 22.3 all-gather.4
  35.2 149.6 all-gather.2
where the time goes:
time: 207 us
  waiting for transfers between devices  136 us (66%)
  blocking collectives  29.6 us (14%)
  matrix products  16.2 us (8%)
  between operations  14.2 us (7%)
  other arithmetic  8.82 us (4%)
    all_gather x1, waiting for transfers between devices, per_device(): image_keys = lax.all_gather(own_image_keys, 'dp', axis=0, tiled=True)  136 us
    all_gather x1, blocking collectives, per_device(): caption_part = lax.all_gather(caption_unit, 'dp', axis=0, tiled=True)  15.3 us
    all_gather x1, blocking collectives, per_device(): image_part = lax.all_gather(image_unit, 'dp', axis=0, tiled=True)  14.3 us
    dot_general x2, matrix products, features(): lax.dot_general(left, right, (((1,), (1,)), ((), ())), preferred_element_...  8.52 us
    dot_general x1, matrix products, per_device(): lax.dot_general(image_store, text_store, (((0,), (0,)), ((), ())), prefer...  7.67 us
  transfers between devices with their start and end apart: 2, of which 1 were waited for; matrix products, arithmetic and copies ran while one was open for 4% of the time, Pallas kernels for 0%

commit v1 on v0

v1 whole, which is shorter than its diff:
```python
import functools
import math

import jax
import jax.numpy as jnp
from jax import lax
from jax.experimental import pallas as pl
from jax.experimental.pallas import tpu as pltpu
from jax.sharding import PartitionSpec as P

MESH = pl.DeviceIdType.MESH
EPS = 1e-06


def unit_rows(wide):
    return wide * lax.rsqrt(jnp.sum(wide * wide, axis=-1, keepdims=True) + EPS)


def diagonal(size):
    return lax.broadcasted_iota(jnp.int32, (size, size), 0) == lax.broadcasted_iota(
        jnp.int32, (size, size), 1
    )


def scaled_keys(marks_ref, gamma_ref, keys_ref):
    total = marks_ref.shape[0]
    size = min(128, total)

    def step(at, carry):
        rows = pl.ds(pl.multiple_of(at * size, size), size)
        unit = unit_rows(marks_ref[rows, :].astype(jnp.float32))
        gamma = jnp.sum(
            jnp.where(diagonal(size), gamma_ref[:, rows], 0.0), axis=1, keepdims=True
        )
        keys_ref[rows, :] = (unit * gamma).astype(jnp.bfloat16)
        return carry

    lax.fori_loop(0, total // size, step, 0)


def standard_features(keys, units, mean_ref, start, scale):
    rows, pairs = keys.shape[0], units.shape[0]
    inner = lax.dot_general(
        keys, units, (((1,), (1,)), ((), ())), preferred_element_type=jnp.float32
    )
    feats = jnp.exp(inner).astype(jnp.bfloat16).astype(jnp.float32)
    mean = jnp.sum(feats, axis=1, keepdims=True) * (1.0 / pairs)
    dev = feats - mean
    var = jnp.sum(dev * dev, axis=1, keepdims=True) * (1.0 / pairs)
    size = min(128, rows)
    for at in range(0, rows, size):
        mean_ref[:, start + at : start + at + size] = jnp.sum(
            jnp.where(diagonal(size), mean[at : at + size], 0.0), axis=0, keepdims=True
        )
    return (dev * (lax.rsqrt(var + EPS) * scale)).astype(jnp.bfloat16)


def exchange_kernel(
    dp, lm, split, chunks,
    images_ref, captions_ref, order_ref, marks_hbm, gamma_ref, words_hbm, text_gamma_ref,
    f_hbm, g_hbm, image_mean_ref, text_mean_ref,
    u_all, c_all, f_all, g_all, marks, words, keys, text_keys,
    load_sem, out_sem,
    u_send, u_recv, u_mate_send, u_mate_recv,
    c_send, c_recv, c_mate_send, c_mate_recv,
    right_send, left_send, f_recv, g_send, g_recv,
):
    me, lane = lax.axis_index("dp"), lax.axis_index("landmark")
    block = images_ref.shape[0]
    part = block // split
    own = marks.shape[0]
    text_own = words.shape[0]
    pairs = u_all.shape[0]
    rows_each = own // chunks

    load_marks = pltpu.make_async_copy(marks_hbm, marks, load_sem.at[0])
    load_words = pltpu.make_async_copy(words_hbm, words, load_sem.at[1])
    load_marks.start()
    load_words.start()

    barrier = pltpu.get_barrier_semaphore()
    for k in range(1, dp):
        pl.semaphore_signal(
            barrier, inc=1, device_id={"dp": lax.rem(me + k, dp)}, device_id_type=MESH
        )
    for k in range(1, lm):
        pl.semaphore_signal(
            barrier, inc=1, device_id={"landmark": lax.rem(lane + k, lm)}, device_id_type=MESH
        )

    mine = pl.ds(pl.multiple_of(me * block, block), block)
    u_all[mine, :] = unit_rows(images_ref[...].astype(jnp.float32)).astype(jnp.bfloat16)
    picks = (
        lax.broadcasted_iota(jnp.int32, (block, block), 0) == order_ref[...]
    ).astype(jnp.bfloat16)
    paired = lax.dot_general(
        picks, captions_ref[...], (((0,), (0,)), ((), ())), preferred_element_type=jnp.float32
    )
    c_all[mine, :] = unit_rows(paired).astype(jnp.bfloat16)
    pl.semaphore_wait(barrier, dp - 1 + lm - 1)

    side = lax.rem(lane, split)
    mate = lane + 1 - 2 * side

    def half(shard):
        return pl.ds(pl.multiple_of(shard * block + side * part, part), part)

    def other_half(shard):
        return pl.ds(pl.multiple_of(shard * block + (1 - side) * part, part), part)

    def block_copy(buf, send, recv, k, shard, target):
        return pltpu.make_async_remote_copy(
            src_ref=buf.at[half(shard), :], dst_ref=buf.at[half(shard), :],
            send_sem=send.at[k], recv_sem=recv.at[shard],
            device_id={"dp": target}, device_id_type=MESH,
        )

    def mate_copy(buf, send, recv, k, shard, rows):
        return pltpu.make_async_remote_copy(
            src_ref=buf.at[rows, :], dst_ref=buf.at[rows, :],
            send_sem=send.at[k], recv_sem=recv.at[shard],
            device_id={"landmark": mate}, device_id_type=MESH,
        )

    sends = []
    for buf, send, recv in ((u_all, u_send, u_recv), (c_all, c_send, c_recv)):
        for k in range(1, dp):
            copy = block_copy(buf, send, recv, k - 1, me, lax.rem(me + k, dp))
            copy.start()
            sends.append(copy)

    def collect(buf, send, recv, mate_send, mate_recv):
        for k in range(1, dp):
            shard = lax.rem(me + dp - k, dp)
            block_copy(buf, send, recv, k - 1, shard, me).wait_recv()
            if split > 1:
                copy = mate_copy(buf, mate_send, mate_recv, k - 1, shard, half(shard))
                copy.start()
                sends.append(copy)
        if split > 1:
            for k in range(1, dp):
                shard = lax.rem(me + dp - k, dp)
                mate_copy(
                    buf, mate_send, mate_recv, k - 1, shard, other_half(shard)
                ).wait_recv()

    load_marks.wait()
    scaled_keys(marks, gamma_ref, keys)
    load_words.wait()
    scaled_keys(words, text_gamma_ref, text_keys)

    def f_rows(shard, c):
        return pl.ds(pl.multiple_of(shard * own + c * rows_each, rows_each), rows_each)

    def hop(shard, c, send, target):
        return pltpu.make_async_remote_copy(
            src_ref=f_all.at[f_rows(shard, c), :], dst_ref=f_all.at[f_rows(shard, c), :],
            send_sem=send.at[shard, c], recv_sem=f_recv.at[shard, c],
            device_id={"dp": target}, device_id_type=MESH,
        )

    def to_right(shard, c):
        return hop(shard, c, right_send, jnp.minimum(me + 1, dp - 1))

    def to_left(shard, c):
        return hop(shard, c, left_send, jnp.maximum(me - 1, 0))

    collect(u_all, u_send, u_recv, u_mate_send, u_mate_recv)
    for c in range(chunks):
        at = c * rows_each
        f_all[f_rows(me, c), :] = standard_features(
            keys[at : at + rows_each, :], u_all[...], image_mean_ref, at, 1.0
        )

        @pl.when(me < dp - 1)
        def _():
            to_right(me, c).start()

        @pl.when(me > 0)
        def _():
            to_left(me, c).start()

    collect(c_all, c_send, c_recv, c_mate_send, c_mate_recv)
    text_mine = pl.ds(pl.multiple_of(lane * text_own, text_own), text_own)
    g_all[text_mine, :] = standard_features(
        text_keys[...], c_all[...], text_mean_ref, 0, 1.0 / math.sqrt(pairs)
    )

    def g_copy(k, shard, target):
        rows = pl.ds(pl.multiple_of(shard * text_own, text_own), text_own)
        return pltpu.make_async_remote_copy(
            src_ref=g_all.at[rows, :], dst_ref=g_all.at[rows, :],
            send_sem=g_send.at[k], recv_sem=g_recv.at[shard],
            device_id={"landmark": target}, device_id_type=MESH,
        )

    for k in range(1, lm):
        copy = g_copy(k - 1, lane, lax.rem(lane + k, lm))
        copy.start()
        sends.append(copy)

    for d in range(1, dp):
        for c in range(chunks):

            @pl.when(me - d >= 0)
            def _():
                to_left(me - d, c).wait_recv()

                @pl.when(me < dp - 1)
                def _():
                    to_right(me - d, c).start()

            @pl.when(me + d < dp)
            def _():
                to_right(me + d, c).wait_recv()

                @pl.when(me > 0)
                def _():
                    to_left(me + d, c).start()

    for k in range(1, lm):
        shard = lax.rem(lane + lm - k, lm)
        g_copy(k - 1, shard, lane).wait_recv()

    f_out = pltpu.make_async_copy(f_all, f_hbm, out_sem.at[0])
    g_out = pltpu.make_async_copy(g_all, g_hbm, out_sem.at[1])
    f_out.start()
    g_out.start()
    for copy in sends:
        copy.wait_send()
    for shard in range(dp):
        for c in range(chunks):

            @pl.when(jnp.logical_and(shard <= me, me < dp - 1))
            def _():
                to_right(shard, c).wait_send()

            @pl.when(jnp.logical_and(shard >= me, me > 0))
            def _():
                to_left(shard, c).wait_send()

    f_out.wait()
    g_out.wait()


def product_kernel(f_ref, g_ref, image_mean_in, text_mean_in, z_ref, image_mean_ref, text_mean_ref):
    z_ref[...] = lax.dot_general(
        f_ref[...], g_ref[...], (((1,), (1,)), ((), ())), preferred_element_type=jnp.float32
    )

    @pl.when(pl.program_id(0) == 0)
    def _():
        image_mean_ref[...] = image_mean_in[...]
        text_mean_ref[...] = text_mean_in[...]


def per_device(
    images, captions, caption_of, image_landmarks, image_gamma, text_landmarks, text_gamma
):
    dp, lm = lax.axis_size("dp"), lax.axis_size("landmark")
    block, width = images.shape
    text_width = captions.shape[1]
    own, text_own = image_landmarks.shape[0], text_landmarks.shape[0]
    pairs = block * dp
    split = 2 if lm % 2 == 0 else 1
    chunks = max(1, own // 256)
    bf16, f32 = jnp.bfloat16, jnp.float32
    vmem = pl.BlockSpec(memory_space=pltpu.VMEM)
    hbm = pl.BlockSpec(memory_space=pl.ANY)
    dma = pltpu.SemaphoreType.DMA
    f, g, image_mean, text_mean = pl.pallas_call(
        functools.partial(exchange_kernel, dp, lm, split, chunks),
        out_shape=(
            jax.ShapeDtypeStruct((dp * own, pairs), bf16),
            jax.ShapeDtypeStruct((lm * text_own, pairs), bf16),
            jax.ShapeDtypeStruct((1, own), f32),
            jax.ShapeDtypeStruct((1, text_own), f32),
        ),
        in_specs=[vmem, vmem, vmem, hbm, vmem, hbm, vmem],
        out_specs=(hbm, hbm, vmem, vmem),
        scratch_shapes=[
            pltpu.VMEM((pairs, width), bf16),
            pltpu.VMEM((pairs, text_width), bf16),
            pltpu.VMEM((dp * own, pairs), bf16),
            pltpu.VMEM((lm * text_own, pairs), bf16),
            pltpu.VMEM((own, width), bf16),
            pltpu.VMEM((text_own, text_width), bf16),
            pltpu.VMEM((own, width), bf16),
            pltpu.VMEM((text_own, text_width), bf16),
            dma((2,)),
            dma((2,)),
            dma((dp,)), dma((dp,)), dma((dp,)), dma((dp,)),
            dma((dp,)), dma((dp,)), dma((dp,)), dma((dp,)),
            dma((dp, chunks)), dma((dp, chunks)), dma((dp, chunks)),
            dma((lm,)), dma((lm,)),
        ],
        compiler_params=pltpu.CompilerParams(
            collective_id=0, has_side_effects=True, vmem_limit_bytes=40 * 2**20
        ),
        name="exchange",
    )(
        images, captions, caption_of[None, :], image_landmarks, image_gamma[None, :],
        text_landmarks, text_gamma[None, :],
    )
    rows, columns = dp * own, lm * text_own
    tile = math.gcd(rows, 512)
    zstat, image_mean, text_mean = pl.pallas_call(
        product_kernel,
        grid=(rows // tile,),
        out_shape=(
            jax.ShapeDtypeStruct((rows, columns), f32),
            jax.ShapeDtypeStruct((1, own), f32),
            jax.ShapeDtypeStruct((1, text_own), f32),
        ),
        in_specs=[
            pl.BlockSpec((tile, pairs), lambda i: (i, 0)),
            pl.BlockSpec((columns, pairs), lambda i: (0, 0)),
            pl.BlockSpec((1, own), lambda i: (0, 0)),
            pl.BlockSpec((1, text_own), lambda i: (0, 0)),
        ],
        out_specs=(
            pl.BlockSpec((tile, columns), lambda i: (i, 0)),
            pl.BlockSpec((1, own), lambda i: (0, 0)),
            pl.BlockSpec((1, text_own), lambda i: (0, 0)),
        ),
        compiler_params=pltpu.CompilerParams(vmem_limit_bytes=40 * 2**20),
        name="product",
    )(f, g, image_mean, text_mean)
    return (zstat, image_mean[0], text_mean[0])


def solution(mesh):
    in_specs = (
        P(("groups", "dp"), None),
        P(("groups", "dp"), None),
        P(("groups", "dp")),
        P(("landmark", "dp"), None),
        P(("landmark", "dp")),
        P(("dp", "landmark"), None),
        P(("dp", "landmark")),
    )
    out_specs = (
        P(("groups", "landmark"), "dp"),
        P(("groups", "landmark", "dp")),
        P(("groups", "dp", "landmark")),
    )
    return jax.shard_map(
        per_device, mesh=mesh, in_specs=in_specs, out_specs=out_specs, check_vma=False
    )
```

time: 207 us -> 46 us (0.22)
  waiting for transfers between devices: 136 us -> 0 us
  Pallas kernels: 0 us -> 38.8 us
  blocking collectives: 29.6 us -> 0 us
  matrix products: 16.2 us -> 0 us
  between operations: 14.2 us -> 0.66 us
  other arithmetic: 8.82 us -> 0 us
  local copies, waits for them, and re-layouts: 1.9 us -> 6.24 us
    all_gather x2 -> x0, waiting for transfers between devices: 136 us -> none  [the longest x1 136 us: per_device(): image_keys = lax.all_gather(own_image_keys, 'dp', axis=0, tiled=True)]
    pallas_call x0 -> x2, Pallas kernels: none -> 38.8 us  [the longest x1 31 us: per_device(): pl.pallas_call(functools.partial(exchange_kernel, dp, lm, split, chunks),...]
    all_gather x2 -> x0, blocking collectives: 29.6 us -> none  [the longest x1 15.3 us: per_device(): caption_part = lax.all_gather(caption_unit, 'dp', axis=0, tiled=True)]
    dot_general x3 -> x0, matrix products: 16.2 us -> none  [the longest x2 8.52 us: features(): lax.dot_general(left, right, (((1,), (1,)), ((), ())), preferred_element_...]
    unnamed x8 -> x14, local copies, waits for them, and re-layouts: 0.03 us -> 6.24 us
    convert_element_type x4 -> x0, other arithmetic: 4.68 us -> none  [the longest x1 2.55 us: per_device(): (unit_rows(image_landmarks) * image_gamma[:, None]).astype(jnp.bfloat16)]
    reduce_sum x6 -> x0, other arithmetic: 4.07 us -> none  [the longest x4 3.68 us: unit_rows(): jnp.sum(wide * wide, axis=-1, keepdims=True) + 1e-06]
  transfers between devices with their start and end apart: 2 -> 0, of which waited for: 1 -> 0; matrix products, arithmetic and copies ran while one was open for 4% -> 0% of each run, Pallas kernels for 0% -> 0%
where the time goes in v1:
time: 46 us; the launch traced here: 45.7 us
  Pallas kernels  38.8 us (84%)
  local copies, waits for them, and re-layouts  6.24 us (14%)
  between operations  0.66 us (1%)
    pallas_call x1, Pallas kernels, per_device(): pl.pallas_call(functools.partial(exchange_kernel, dp, lm, split, chunks),...  31 us
    pallas_call x1, Pallas kernels, per_device(): pl.pallas_call(product_kernel, grid=(rows // tile,), out_shape=(jax.Shape...  7.73 us
    unnamed x14, local copies, waits for them, and re-layouts  6.24 us

profile of v1, /device:TPU:0, one launch (start us, length us, event | category | flops | bytes accessed | tf_op | source)
XLA Modules:
  0.0 45.7 jit_solution(4400153883214949567)
XLA Ops:
  0.6 0.0 copy-start
  0.6 1.6 %copy-done = bf16[1024,1024]{1,0:T(8,128)(2,1)S(1)} copy-done((bf16[1024,1024]{1,0:T(8,128)(2,1)S(1)}, bf16[1024,1024]{1,0:T(8,128)(2,1)}, u32[]{:S(2)}) %copy-start) | copy-done | bytes 2097176
  2.2 0.0 copy-start.1
  2.2 1.0 %copy-done.1 = bf16[256,768]{1,0:T(8,128)(2,1)S(1)} copy-done((bf16[256,768]{1,0:T(8,128)(2,1)S(1)}, bf16[256,768]{1,0:T(8,128)(2,1)}, u32[]{:S(2)}) %copy-start.1) | copy-done | bytes 393240
  3.2 0.0 copy-start.2
  3.2 0.8 %copy-done.2 = bf16[32,1024]{1,0:T(8,128)(2,1)S(1)} copy-done((bf16[32,1024]{1,0:T(8,128)(2,1)S(1)}, bf16[32,1024]{1,0:T(8,128)(2,1)}, u32[]{:S(2)}) %copy-start.2) | copy-done | bytes 65560
  4.1 0.0 copy-start.3
  4.1 0.8 %copy-done.3 = bf16[32,768]{1,0:T(8,128)(2,1)S(1)} copy-done((bf16[32,768]{1,0:T(8,128)(2,1)S(1)}, bf16[32,768]{1,0:T(8,128)(2,1)}, u32[]{:S(2)}) %copy-start.3) | copy-done | bytes 49176
  4.9 0.0 copy-start.4
  4.9 0.7 %copy-done.4 = f32[1024]{0:T(1024)S(1)} copy-done((f32[1024]{0:T(1024)S(1)}, f32[1024]{0:T(1024)}, u32[]{:S(2)}) %copy-start.4) | copy-done | bytes 4120
  5.5 0.0 copy-start.5
  5.5 0.7 %copy-done.5 = f32[256]{0:T(256)S(1)} copy-done((f32[256]{0:T(256)S(1)}, f32[256]{0:T(256)}, u32[]{:S(2)}) %copy-start.5) | copy-done | bytes 1048
  6.2 0.0 copy-start.6
  6.2 0.7 %copy-done.6 = s32[32]{0:T(128)S(1)} copy-done((s32[32]{0:T(128)S(1)}, s32[32]{0:T(128)}, u32[]{:S(2)}) %copy-start.6) | copy-done | bytes 152
  6.9 31.0 %exchange.1 = (bf16[4096,128]{1,0:T(8,128)(2,1)S(1)}, bf16[1024,128]{1,0:T(8,128)(2,1)S(1)}, f32[1,1024]{1,0:T(1,128)S(1)}, f32[1,256]{1,0:T(1,128)S(1)}) custom-call(bf16[32,1024]{1,0:T(8,128)(2,1)S(1)} %copy-done.2, bf16[32,768]{1,0:T(8,128)(2,1)S(1)} %copy-done.3, s32[1,32]{1,0:T(1,128)S(1)} %bitcast.7, bf16[1024,1024]{1,0:T(8,128)(2,1)S(1)} %copy-done, ...), custom_call_target="tpu_custom_call" | custom-call | tf_op jit(solution)/shard_map/exchange/pallas_call | solution.py:271
  37.9 7.7 %product.1 = (f32[4096,1024]{1,0:T(8,128)}, f32[1,1024]{1,0:T(1,128)}, f32[1,256]{1,0:T(1,128)}) custom-call(bf16[4096,128]{1,0:T(8,128)(2,1)S(1)} %get-tuple-element.10.f_ref, bf16[1024,128]{1,0:T(8,128)(2,1)S(1)} %get-tuple-element.11.g_ref, f32[1,1024]{1,0:T(1,128)S(1)} %get-tuple-element.12.image_mean_in, f32[1,256]{1,0:T(1,128)S(1)} %get-tuple-element.13.text_mean_in), custom_call_target="tpu_custom_call" | custom-call | tf_op jit(solution)/shard_map/product/pallas_call | solution.py:307
Async XLA Ops:
  0.6 1.6 %copy-start = (bf16[1024,1024]{1,0:T(8,128)(2,1)S(1)}, bf16[1024,1024]{1,0:T(8,128)(2,1)}, u32[]{:S(2)}) copy-start(bf16[1024,1024]{1,0:T(8,128)(2,1)} %marks_hbm.1) | copy-start | bytes 6291460
  2.2 1.0 %copy-start.1 = (bf16[256,768]{1,0:T(8,128)(2,1)S(1)}, bf16[256,768]{1,0:T(8,128)(2,1)}, u32[]{:S(2)}) copy-start(bf16[256,768]{1,0:T(8,128)(2,1)} %words_hbm.1) | copy-start | bytes 1179652
  3.2 0.8 %copy-start.2 = (bf16[32,1024]{1,0:T(8,128)(2,1)S(1)}, bf16[32,1024]{1,0:T(8,128)(2,1)}, u32[]{:S(2)}) copy-start(bf16[32,1024]{1,0:T(8,128)(2,1)} %images_ref.1) | copy-start | bytes 196612
  4.1 0.8 %copy-start.3 = (bf16[32,768]{1,0:T(8,128)(2,1)S(1)}, bf16[32,768]{1,0:T(8,128)(2,1)}, u32[]{:S(2)}) copy-start(bf16[32,768]{1,0:T(8,128)(2,1)} %captions_ref.1) | copy-start | bytes 147460
  4.9 0.7 %copy-start.4 = (f32[1024]{0:T(1024)S(1)}, f32[1024]{0:T(1024)}, u32[]{:S(2)}) copy-start(f32[1024]{0:T(1024)} %param.11) | copy-start | bytes 12292
  5.5 0.7 %copy-start.5 = (f32[256]{0:T(256)S(1)}, f32[256]{0:T(256)}, u32[]{:S(2)}) copy-start(f32[256]{0:T(256)} %param.13) | copy-start | bytes 3076
  6.2 0.7 %copy-start.6 = (s32[32]{0:T(128)S(1)}, s32[32]{0:T(128)}, u32[]{:S(2)}) copy-start(s32[32]{0:T(128)} %param.9) | copy-start | bytes 388

commit v2 on v1

--- a/solution.py
+++ b/solution.py
@@ -57,10 +57,11 @@
 
 def exchange_kernel(
     dp, lm, split, chunks,
-    images_ref, captions_ref, order_ref, marks_hbm, gamma_ref, words_hbm, text_gamma_ref,
-    f_hbm, g_hbm, image_mean_ref, text_mean_ref,
-    u_all, c_all, f_all, g_all, marks, words, keys, text_keys,
-    load_sem, out_sem,
+    images_hbm, captions_hbm, order_hbm, marks_hbm, gamma_hbm, words_hbm, text_gamma_hbm,
+    f_all, g_all, image_mean_ref, text_mean_ref,
+    images_ref, captions_ref, order_ref, marks, gamma_ref, words, text_gamma_ref,
+    u_all, c_all, keys, text_keys,
+    load_sem,
     u_send, u_recv, u_mate_send, u_mate_recv,
     c_send, c_recv, c_mate_send, c_mate_recv,
     right_send, left_send, f_recv, g_send, g_recv,
@@ -73,10 +74,16 @@
     pairs = u_all.shape[0]
     rows_each = own // chunks
 
-    load_marks = pltpu.make_async_copy(marks_hbm, marks, load_sem.at[0])
-    load_words = pltpu.make_async_copy(words_hbm, words, load_sem.at[1])
-    load_marks.start()
-    load_words.start()
+    loads = [
+        pltpu.make_async_copy(src, dst, load_sem.at[at])
+        for at, (src, dst) in enumerate((
+            (images_hbm, images_ref), (marks_hbm, marks), (gamma_hbm, gamma_ref),
+            (captions_hbm, captions_ref), (order_hbm, order_ref),
+            (words_hbm, words), (text_gamma_hbm, text_gamma_ref),
+        ))
+    ]
+    for load in loads:
+        load.start()
 
     barrier = pltpu.get_barrier_semaphore()
     for k in range(1, dp):
@@ -89,14 +96,8 @@
         )
 
     mine = pl.ds(pl.multiple_of(me * block, block), block)
+    loads[0].wait()
     u_all[mine, :] = unit_rows(images_ref[...].astype(jnp.float32)).astype(jnp.bfloat16)
-    picks = (
-        lax.broadcasted_iota(jnp.int32, (block, block), 0) == order_ref[...]
-    ).astype(jnp.bfloat16)
-    paired = lax.dot_general(
-        picks, captions_ref[...], (((0,), (0,)), ((), ())), preferred_element_type=jnp.float32
-    )
-    c_all[mine, :] = unit_rows(paired).astype(jnp.bfloat16)
     pl.semaphore_wait(barrier, dp - 1 + lm - 1)
 
     side = lax.rem(lane, split)
@@ -123,11 +124,14 @@
         )
 
     sends = []
-    for buf, send, recv in ((u_all, u_send, u_recv), (c_all, c_send, c_recv)):
+
+    def spread(buf, send, recv):
         for k in range(1, dp):
             copy = block_copy(buf, send, recv, k - 1, me, lax.rem(me + k, dp))
             copy.start()
             sends.append(copy)
+
+    spread(u_all, u_send, u_recv)
 
     def collect(buf, send, recv, mate_send, mate_recv):
         for k in range(1, dp):
@@ -144,10 +148,18 @@
                     buf, mate_send, mate_recv, k - 1, shard, other_half(shard)
                 ).wait_recv()
 
-    load_marks.wait()
+    loads[1].wait()
+    loads[2].wait()
     scaled_keys(marks, gamma_ref, keys)
-    load_words.wait()
-    scaled_keys(words, text_gamma_ref, text_keys)
+    loads[3].wait()
+    loads[4].wait()
+    picks = (
+        lax.broadcasted_iota(jnp.int32, (block, block), 0) == order_ref[...]
+    ).astype(jnp.bfloat16)
+    paired = lax.dot_general(
+        picks, captions_ref[...], (((0,), (0,)), ((), ())), preferred_element_type=jnp.float32
+    )
+    c_all[mine, :] = unit_rows(paired).astype(jnp.bfloat16)
 
     def f_rows(shard, c):
         return pl.ds(pl.multiple_of(shard * own + c * rows_each, rows_each), rows_each)
@@ -166,6 +178,7 @@
         return hop(shard, c, left_send, jnp.maximum(me - 1, 0))
 
     collect(u_all, u_send, u_recv, u_mate_send, u_mate_recv)
+    spread(c_all, c_send, c_recv)
     for c in range(chunks):
         at = c * rows_each
         f_all[f_rows(me, c), :] = standard_features(
@@ -180,6 +193,9 @@
         def _():
             to_left(me, c).start()
 
+    loads[5].wait()
+    loads[6].wait()
+    scaled_keys(words, text_gamma_ref, text_keys)
     collect(c_all, c_send, c_recv, c_mate_send, c_mate_recv)
     text_mine = pl.ds(pl.multiple_of(lane * text_own, text_own), text_own)
     g_all[text_mine, :] = standard_features(
@@ -222,10 +238,6 @@
         shard = lax.rem(lane + lm - k, lm)
         g_copy(k - 1, shard, lane).wait_recv()
 
-    f_out = pltpu.make_async_copy(f_all, f_hbm, out_sem.at[0])
-    g_out = pltpu.make_async_copy(g_all, g_hbm, out_sem.at[1])
-    f_out.start()
-    g_out.start()
     for copy in sends:
         copy.wait_send()
     for shard in range(dp):
@@ -239,19 +251,36 @@
             def _():
                 to_left(shard, c).wait_send()
 
-    f_out.wait()
-    g_out.wait()
-
-
-def product_kernel(f_ref, g_ref, image_mean_in, text_mean_in, z_ref, image_mean_ref, text_mean_ref):
-    z_ref[...] = lax.dot_general(
-        f_ref[...], g_ref[...], (((1,), (1,)), ((), ())), preferred_element_type=jnp.float32
-    )
-
-    @pl.when(pl.program_id(0) == 0)
-    def _():
-        image_mean_ref[...] = image_mean_in[...]
-        text_mean_ref[...] = text_mean_in[...]
+
+def product_kernel(
+    tile, slots, f_ref, g_ref, image_mean_in, text_mean_in,
+    z_hbm, image_mean_ref, text_mean_ref, buf, sem,
+):
+    steps = f_ref.shape[0] // tile
+
+    def out(at):
+        slot = lax.rem(at, slots)
+        rows = pl.ds(pl.multiple_of(at * tile, tile), tile)
+        return pltpu.make_async_copy(buf.at[slot], z_hbm.at[rows, :], sem.at[slot])
+
+    def step(at, carry):
+        @pl.when(at >= slots)
+        def _():
+            out(at - slots).wait()
+
+        rows = pl.ds(pl.multiple_of(at * tile, tile), tile)
+        buf[lax.rem(at, slots)] = lax.dot_general(
+            f_ref[rows, :], g_ref[...], (((1,), (1,)), ((), ())),
+            preferred_element_type=jnp.float32,
+        )
+        out(at).start()
+        return carry
+
+    lax.fori_loop(0, steps, step, 0)
+    image_mean_ref[...] = image_mean_in[...]
+    text_mean_ref[...] = text_mean_in[...]
+    for at in range(max(0, steps - slots), steps):
+        out(jnp.int32(at)).wait()
 
 
 def per_device(
@@ -263,10 +292,10 @@
     own, text_own = image_landmarks.shape[0], text_landmarks.shape[0]
     pairs = block * dp
     split = 2 if lm % 2 == 0 else 1
-    chunks = max(1, own // 256)
+    chunks = max(1, own // 128)
     bf16, f32 = jnp.bfloat16, jnp.float32
     vmem = pl.BlockSpec(memory_space=pltpu.VMEM)
-    hbm = pl.BlockSpec(memory_space=pl.ANY)
+    hbm = pl.BlockSpec(memory_space=pltpu.HBM)
     dma = pltpu.SemaphoreType.DMA
     f, g, image_mean, text_mean = pl.pallas_call(
         functools.partial(exchange_kernel, dp, lm, split, chunks),
@@ -276,19 +305,21 @@
             jax.ShapeDtypeStruct((1, own), f32),
             jax.ShapeDtypeStruct((1, text_own), f32),
         ),
-        in_specs=[vmem, vmem, vmem, hbm, vmem, hbm, vmem],
-        out_specs=(hbm, hbm, vmem, vmem),
+        in_specs=[hbm] * 7,
+        out_specs=(vmem, vmem, vmem, vmem),
         scratch_shapes=[
+            pltpu.VMEM((block, width), bf16),
+            pltpu.VMEM((block, text_width), bf16),
+            pltpu.VMEM((1, block), jnp.int32),
+            pltpu.VMEM((own, width), bf16),
+            pltpu.VMEM((1, own), f32),
+            pltpu.VMEM((text_own, text_width), bf16),
+            pltpu.VMEM((1, text_own), f32),
             pltpu.VMEM((pairs, width), bf16),
             pltpu.VMEM((pairs, text_width), bf16),
-            pltpu.VMEM((dp * own, pairs), bf16),
-            pltpu.VMEM((lm * text_own, pairs), bf16),
             pltpu.VMEM((own, width), bf16),
             pltpu.VMEM((text_own, text_width), bf16),
-            pltpu.VMEM((own, width), bf16),
-            pltpu.VMEM((text_own, text_width), bf16),
-            dma((2,)),
-            dma((2,)),
+            dma((7,)),
             dma((dp,)), dma((dp,)), dma((dp,)), dma((dp,)),
             dma((dp,)), dma((dp,)), dma((dp,)), dma((dp,)),
             dma((dp, chunks)), dma((dp, chunks)), dma((dp, chunks)),
@@ -299,30 +330,27 @@
         ),
         name="exchange",
     )(
-        images, captions, caption_of[None, :], image_landmarks, image_gamma[None, :],
-        text_landmarks, text_gamma[None, :],
+        *(
+            pltpu.with_memory_space_constraint(value, pltpu.HBM)
+            for value in (
+                images, captions, caption_of[None, :], image_landmarks, image_gamma[None, :],
+                text_landmarks, text_gamma[None, :],
+            )
+        )
     )
     rows, columns = dp * own, lm * text_own
-    tile = math.gcd(rows, 512)
+    tile = math.gcd(rows, 256)
+    slots = min(4, rows // tile)
     zstat, image_mean, text_mean = pl.pallas_call(
-        product_kernel,
-        grid=(rows // tile,),
+        functools.partial(product_kernel, tile, slots),
         out_shape=(
             jax.ShapeDtypeStruct((rows, columns), f32),
             jax.ShapeDtypeStruct((1, own), f32),
             jax.ShapeDtypeStruct((1, text_own), f32),
         ),
-        in_specs=[
-            pl.BlockSpec((tile, pairs), lambda i: (i, 0)),
-            pl.BlockSpec((columns, pairs), lambda i: (0, 0)),
-            pl.BlockSpec((1, own), lambda i: (0, 0)),
-            pl.BlockSpec((1, text_own), lambda i: (0, 0)),
-        ],
-        out_specs=(
-            pl.BlockSpec((tile, columns), lambda i: (i, 0)),
-            pl.BlockSpec((1, own), lambda i: (0, 0)),
-            pl.BlockSpec((1, text_own), lambda i: (0, 0)),
-        ),
+        in_specs=[vmem] * 4,
+        out_specs=(hbm, vmem, vmem),
+        scratch_shapes=[pltpu.VMEM((slots, tile, columns), f32), dma((slots,))],
         compiler_params=pltpu.CompilerParams(vmem_limit_bytes=40 * 2**20),
         name="product",
     )(f, g, image_mean, text_mean)

time: 46 us -> 38.7 us (0.84)
  local copies, waits for them, and re-layouts: 6.24 us -> 0 us
  Pallas kernels: 38.8 us -> 37.9 us
    unnamed x14 -> x0, local copies, waits for them, and re-layouts: 6.24 us -> none
    pallas_call x1, Pallas kernels: 7.73 us -> 6.76 us  [per_device(): pl.pallas_call(functools.partial(product_kernel, tile, slots), out_shape=...]
where the time goes in v2:
time: 38.7 us; the launch traced here: 38.6 us
  Pallas kernels  37.9 us (98%)
  between operations  0.64 us (2%)
    pallas_call x1, Pallas kernels, per_device(): pl.pallas_call(functools.partial(exchange_kernel, dp, lm, split, chunks),...  31.2 us
    pallas_call x1, Pallas kernels, per_device(): pl.pallas_call(functools.partial(product_kernel, tile, slots), out_shape=...  6.76 us

profile of v2, /device:TPU:0, one launch (start us, length us, event | category | flops | bytes accessed | tf_op | source)
XLA Modules:
  0.0 38.6 jit_solution(4317002021846846210)
XLA Ops:
  0.6 31.2 %exchange.1 = (bf16[4096,128]{1,0:T(8,128)(2,1)S(1)}, bf16[1024,128]{1,0:T(8,128)(2,1)S(1)}, f32[1,1024]{1,0:T(1,128)S(1)}, f32[1,256]{1,0:T(1,128)S(1)}) custom-call(bf16[32,1024]{1,0:T(8,128)(2,1)} %images_hbm.1, bf16[32,768]{1,0:T(8,128)(2,1)} %captions_hbm.1, s32[1,32]{1,0:T(1,128)} %bitcast.7, bf16[1024,1024]{1,0:T(8,128)(2,1)} %marks_hbm.1, ...), custom_call_target="tpu_custom_call" | custom-call | tf_op jit(solution)/shard_map/exchange/pallas_call | solution.py:300
  31.8 6.8 %product.1 = (f32[4096,1024]{1,0:T(8,128)}, f32[1,1024]{1,0:T(1,128)}, f32[1,256]{1,0:T(1,128)}) custom-call(bf16[4096,128]{1,0:T(8,128)(2,1)S(1)} %get-tuple-element.10.f_ref, bf16[1024,128]{1,0:T(8,128)(2,1)S(1)} %get-tuple-element.11.g_ref, f32[1,1024]{1,0:T(1,128)S(1)} %get-tuple-element.12.image_mean_in, f32[1,256]{1,0:T(1,128)S(1)} %get-tuple-element.13.text_mean_in), custom_call_target="tpu_custom_call" | custom-call | tf_op jit(solution)/shard_map/product/pallas_call | solution.py:344

commit v3 on v2

--- a/solution.py
+++ b/solution.py
@@ -148,9 +148,6 @@
                     buf, mate_send, mate_recv, k - 1, shard, other_half(shard)
                 ).wait_recv()
 
-    loads[1].wait()
-    loads[2].wait()
-    scaled_keys(marks, gamma_ref, keys)
     loads[3].wait()
     loads[4].wait()
     picks = (
@@ -160,7 +157,10 @@
         picks, captions_ref[...], (((0,), (0,)), ((), ())), preferred_element_type=jnp.float32
     )
     c_all[mine, :] = unit_rows(paired).astype(jnp.bfloat16)
-
+    spread(c_all, c_send, c_recv)
+    loads[1].wait()
+    loads[2].wait()
+    scaled_keys(marks, gamma_ref, keys)
     def f_rows(shard, c):
         return pl.ds(pl.multiple_of(shard * own + c * rows_each, rows_each), rows_each)
 
@@ -178,7 +178,6 @@
         return hop(shard, c, left_send, jnp.maximum(me - 1, 0))
 
     collect(u_all, u_send, u_recv, u_mate_send, u_mate_recv)
-    spread(c_all, c_send, c_recv)
     for c in range(chunks):
         at = c * rows_each
         f_all[f_rows(me, c), :] = standard_features(
@@ -292,7 +291,7 @@
     own, text_own = image_landmarks.shape[0], text_landmarks.shape[0]
     pairs = block * dp
     split = 2 if lm % 2 == 0 else 1
-    chunks = max(1, own // 128)
+    chunks = max(1, own // 256)
     bf16, f32 = jnp.bfloat16, jnp.float32
     vmem = pl.BlockSpec(memory_space=pltpu.VMEM)
     hbm = pl.BlockSpec(memory_space=pltpu.HBM)

time: 38.7 us -> 38.2 us (0.987)
  Pallas kernels: 37.9 us -> 37.4 us
    pallas_call x1, Pallas kernels: 31.2 us -> 30.7 us  [per_device(): pl.pallas_call(functools.partial(exchange_kernel, dp, lm, split, chunks),...]
where the time goes in v3:
time: 38.2 us; the launch traced here: 38.1 us
  Pallas kernels  37.4 us (98%)
  between operations  0.64 us (2%)
    pallas_call x1, Pallas kernels, per_device(): pl.pallas_call(functools.partial(exchange_kernel, dp, lm, split, chunks),...  30.7 us
    pallas_call x1, Pallas kernels, per_device(): pl.pallas_call(functools.partial(product_kernel, tile, slots), out_shape=...  6.76 us

profile of v3, /device:TPU:0, one launch (start us, length us, event | category | flops | bytes accessed | tf_op | source)
XLA Modules:
  0.0 38.1 jit_solution(13395510368072005951)
XLA Ops:
  0.6 30.7 %exchange.1 = (bf16[4096,128]{1,0:T(8,128)(2,1)S(1)}, bf16[1024,128]{1,0:T(8,128)(2,1)S(1)}, f32[1,1024]{1,0:T(1,128)S(1)}, f32[1,256]{1,0:T(1,128)S(1)}) custom-call(bf16[32,1024]{1,0:T(8,128)(2,1)} %images_hbm.1, bf16[32,768]{1,0:T(8,128)(2,1)} %captions_hbm.1, s32[1,32]{1,0:T(1,128)} %bitcast.7, bf16[1024,1024]{1,0:T(8,128)(2,1)} %marks_hbm.1, ...), custom_call_target="tpu_custom_call" | custom-call | tf_op jit(solution)/shard_map/exchange/pallas_call | solution.py:299
  31.3 6.8 %product.1 = (f32[4096,1024]{1,0:T(8,128)}, f32[1,1024]{1,0:T(1,128)}, f32[1,256]{1,0:T(1,128)}) custom-call(bf16[4096,128]{1,0:T(8,128)(2,1)S(1)} %get-tuple-element.10.f_ref, bf16[1024,128]{1,0:T(8,128)(2,1)S(1)} %get-tuple-element.11.g_ref, f32[1,1024]{1,0:T(1,128)S(1)} %get-tuple-element.12.image_mean_in, f32[1,256]{1,0:T(1,128)S(1)} %get-tuple-element.13.text_mean_in), custom_call_target="tpu_custom_call" | custom-call | tf_op jit(solution)/shard_map/product/pallas_call | solution.py:343
